TPU v7x, 32 devices: a whole 2x2x4 slice. The times are simulated.
32 devices in a mesh: batch: 2 (over x), seq: 4 (over y, core), mp: 4 (over z).
Axes of the slice: x: 2, y: 2, z: 4, core: 2. Of those that a mesh axis runs over, the one named last changes fastest.
Arguments:
- context: bfloat16 [1024, 6144], P(('batch', 'seq'), 'mp'), may hold values from -0.25 to 0.25
- cotangent: bfloat16 [1024, 6144], P(('batch', 'seq'), 'mp'), may hold values from -6 to 6
- out_weight: bfloat16 [6144, 6144], P(None, 'mp'), may hold values from -0.078125 to 0.078125
Outputs:
- grad_weight: float32 [6144, 6144], P(('batch', 'seq'), 'mp')
- grad_context: bfloat16 [1024, 6144], P(('batch', 'seq'), 'mp')
All inputs are finite; a program needn't handle non-finite values.
Results may differ from a plain program's by a relative error of at most 0.001.
Values may be sent and summed in bfloat16 or wider, within the bound.
A program may use at most 64 MiB of HBM per device.

v0:
```python
import jax
import jax.numpy as jnp
from jax import lax
from jax.sharding import PartitionSpec as P


def shards(context, cotangent, out_weight):
    groups = lax.axis_size(("batch", "seq"))
    members = lax.axis_size("mp")
    split_rows = lax.all_to_all(context, "mp", split_axis=0, concat_axis=1, tiled=True)
    block_rows = lax.all_to_all(
        split_rows, ("batch", "seq"), split_axis=1, concat_axis=0, tiled=True
    )
    feature_block = lax.all_gather(block_rows, "mp", axis=0, tiled=True)
    all_cotangent = lax.all_gather(cotangent, ("batch", "seq"), axis=0, tiled=True)
    share = split_rows.shape[0]
    shaped_context = feature_block.reshape(members, groups, share, feature_block.shape[1])
    shaped_cotangent = all_cotangent.reshape(groups, members, share, all_cotangent.shape[1])
    grad_weight = lax.dot_general(
        shaped_context,
        shaped_cotangent,
        (((0, 1, 2), (1, 0, 2)), ((), ())),
        preferred_element_type=jnp.float32,
    )
    partial_input = lax.dot_general(
        cotangent, out_weight, (((1,), (1,)), ((), ())), preferred_element_type=jnp.float32
    )
    grad_context = lax.psum_scatter(partial_input, "mp", scatter_dimension=1, tiled=True).astype(
        jnp.bfloat16
    )
    return (grad_weight, grad_context)


def solution(mesh):
    return jax.shard_map(
        shards,
        mesh=mesh,
        in_specs=(P(("batch", "seq"), "mp"), P(("batch", "seq"), "mp"), P(None, "mp")),
        out_specs=(P(("batch", "seq"), "mp"), P(("batch", "seq"), "mp")),
        check_vma=False,
    )
```

profile of v0, /device:TPU:16, one launch (start us, length us, event | category | flops | bytes accessed | tf_op | source)
XLA Modules:
  0.0 174.7 jit_solution(15021152544623179522)
XLA Ops:
  7.2 0.0 copy-start
  7.2 0.0 all-gather.3.cloned.1.call-start
  7.2 14.3 %all_to_all.35 = bf16[4,32,1536]{2,1,0:T(8,128)(2,1)S(1)} all-to-all(bf16[4,32,1536]{2,1,0:T(8,128)(2,1)} %bitcast.16), channel_id=1, replica_groups=mesh['batch'=2,'seq'=4,'mp'=4] {'mp'}, dimensions={0} | all-to-all | bytes 786432 | tf_op jit(solution)/shard_map/all_to_all | solution.py:10
  21.5 0.3 copy.10
  21.8 0.1 all_to_all.29
  21.9 0.1 copy.11
  22.0 11.6 %all_to_all.36 = bf16[32,8,768]{2,0,1:T(8,128)(2,1)} all-to-all(bf16[32,8,768]{2,0,1:T(8,128)(2,1)S(1)} %copy.11), channel_id=1, replica_groups=mesh['batch'=2,'seq'=4,'mp'=4] {'batch','seq'}, dimensions={1} | all-to-all | bytes 786432 | tf_op jit(solution)/shard_map/all_to_all | solution.py:11
  33.6 0.0 all-gather.3.cloned.1.call-update
  33.7 0.0 all-gather.5.cloned.1.call-start
  33.7 0.7 all-gather.5.cloned.1.call-update
  34.4 0.0 reduce-scatter.2.cloned.1.call-start
  34.5 0.0 copy-done
  34.5 14.2 %fusion.1 = f32[128,6144]{1,0:T(8,128)} fusion(bf16[128,1536]{1,0:T(8,128)(2,1)S(1)} %copy-done, bf16[6144,1536]{1,0:T(8,128)(2,1)} %param.5), kind=kOutput, calls=%fused_computation.2 | convolution fusion | flops 2415919104 | bytes 22413312 | tf_op jit(solution)/shard_map/dot_general | solution.py:25
  48.7 0.0 reduce-scatter.2.cloned.1.call-update
  48.7 20.8 %all-gather.3.cloned.1.call-done = bf16[1024,768]{1,0:T(8,128)(2,1)} async-done(((bf16[256,768]{1,0:T(8,128)(2,1)}), bf16[1024,768]{1,0:T(8,128)(2,1)}) %all-gather.3.cloned.1.call-update) | async-done | bytes 1572880 | tf_op jit(solution)/shard_map/all_gather | solution.py:14
  69.5 34.1 %all-gather.5.cloned.1.call-done = bf16[1024,1536]{1,0:T(8,128)(2,1)} async-done(((bf16[128,1536]{1,0:T(8,128)(2,1)}), bf16[1024,1536]{1,0:T(8,128)(2,1)}) %all-gather.5.cloned.1.call-update) | async-done | bytes 3145744 | tf_op jit(solution)/shard_map/all_gather | solution.py:15
  103.6 7.2 %convolution_bitcast_fusion = f32[768,1536]{1,0:T(8,128)} fusion(bf16[4,8,32,768]{3,2,1,0:T(8,128)(2,1)} %bitcast.18, bf16[8,4,32,1536]{3,2,1,0:T(8,128)(2,1)} %bitcast.17), kind=kOutput, calls=%fused_computation | convolution fusion | flops 2415919104 | bytes 9437184 | tf_op jit(solution)/shard_map/dot_general | solution.py:19
  110.8 55.5 %reduce-scatter.2.cloned.1.call-done = f32[128,1536]{1,0:T(8,128)} async-done(((f32[128,6144]{1,0:T(8,128)}), f32[128,1536]{1,0:T(8,128)}) %reduce-scatter.2.cloned.1.call-update) | async-done | bytes 786448 | tf_op jit(solution)/shard_map/reduce_scatter | solution.py:28
  166.2 1.9 %convert_element_type.3 = bf16[128,1536]{1,0:T(8,128)(2,1)} convert(f32[128,1536]{1,0:T(8,128)} %reduce-scatter.2.cloned.1.call-done) | non-fusion elementwise | flops 196608 | bytes 1179648 | tf_op jit(solution)/shard_map/convert_element_type | solution.py:28
Async XLA Ops:
  7.2 27.3 %copy-start = (bf16[128,1536]{1,0:T(8,128)(2,1)S(1)}, bf16[128,1536]{1,0:T(8,128)(2,1)}, u32[]{:S(2)}) copy-start(bf16[128,1536]{1,0:T(8,128)(2,1)} %param.4) | copy-start | bytes 1179652
  7.2 62.3 %all-gather.3.cloned.1.call-start = ((), (), s32[]{:S(2)}) async-start(), calls=%async_computation.3 | async-start | bytes 1966080 | tf_op jit(solution)/shard_map/all_gather | solution.py:14
  33.7 69.9 %all-gather.5.cloned.1.call-start = ((), (), s32[]{:S(2)}) async-start(), calls=%async_computation.4 | async-start | bytes 3538944 | tf_op jit(solution)/shard_map/all_gather | solution.py:15
  34.4 131.8 %reduce-scatter.2.cloned.1.call-start = ((), (), s32[]{:S(2)}) async-start(), calls=%async_computation.5 | async-start | bytes 3932160 | tf_op jit(solution)/shard_map/reduce_scatter | solution.py:28
Sparse Core Ops, SparseCore 0:
  33.8 35.6 all-gather.2
  71.4 32.1 all-gather.4
  105.9 60.3 reduce-scatter.1
where the time goes:
time: 177 us; the launch traced here: 175 us
  waiting for transfers between devices  111 us (63%)
  blocking collectives  25.9 us (15%)
  matrix products  21.4 us (12%)
  between operations  13.8 us (8%)
  other arithmetic  1.92 us (1%)
    reduce_scatter x1, waiting for transfers between devices, shards(): lax.psum_scatter(partial_input, 'mp', scatter_dimension=1, tiled=True)  55.5 us
    all_gather x1, waiting for transfers between devices, shards(): lax.all_gather(cotangent, ('batch', 'seq'), axis=0, tiled=True)  34.1 us
    all_gather x1, waiting for transfers between devices, shards(): feature_block = lax.all_gather(block_rows, 'mp', axis=0, tiled=True)  20.8 us
    all_to_all x1, blocking collectives, shards(): lax.all_to_all(context, 'mp', split_axis=0, concat_axis=1, tiled=True)  14.3 us
    dot_general x1, matrix products, shards(): lax.dot_general(cotangent, out_weight, (((1,), (1,)), ((), ())), preferre...  14.2 us
    all_to_all x1, blocking collectives, shards(): lax.all_to_all(split_rows, ('batch', 'seq'), split_axis=1, concat_axis=0,...  11.6 us
    dot_general x1, matrix products, shards(): lax.dot_general(shaped_context, shaped_cotangent, (((0, 1, 2), (1, 0, 2))...  7.19 us
  transfers between devices with their start and end apart: 3, of which 3 were waited for; matrix products, arithmetic and copies ran while one was open for 12% of the time, Pallas kernels for 0%

commit v1 on v0

v1 whole, which is shorter than its diff:
```python
import functools

import jax
import jax.numpy as jnp
from jax import lax
from jax.experimental import pallas as pl
from jax.experimental.pallas import tpu as pltpu
from jax.sharding import PartitionSpec as P

MESH = pl.DeviceIdType.MESH
CHUNKS = 2


def tile_of(width):
    return 256 if width % 256 == 0 else 128


def kernel(
    B, S, M,
    ctx, cot, w, gw, gc,
    zctx, cotall, ctxall, ctxt, part, rup, rdn, wbuf,
    wsem, zr, zu, zd, cs, cr, ks, kf, kr, pus, pds, pur, pdr,
):
    G = B * S
    Q = G // M
    T, width = cot.shape
    rows = T // CHUNKS
    half = S // 2
    b, s, m = lax.axis_index("batch"), lax.axis_index("seq"), lax.axis_index("mp")
    bs = b * S + s
    parity = lax.rem(s, 2)
    partner = (b, s + 1 - 2 * parity, m)
    partner_bs = b * S + s + 1 - 2 * parity
    above, below = (b, s, m + 1), (b, s, m - 1)

    depth = ctxall.shape[2]

    def piece_of(ref, h):
        return ref.at[:, pl.ds(h * depth, depth)] if len(ctx.shape) == 2 else ref.at[h]

    def plane(index):
        return (index // S, lax.rem(index, S), m)

    def remote(src, dst, send, recv, device):
        return pltpu.make_async_remote_copy(
            src_ref=src, dst_ref=dst, send_sem=send, recv_sem=recv,
            device_id=device, device_id_type=MESH,
        )

    order = []
    for step in range((M + 1) // 2):
        order.append(M - 1 - step)
        if step != M - 1 - step:
            order.append(step)

    def load(position):
        k = order[position]
        return pltpu.make_async_copy(
            w.at[pl.ds(k * width, width), :], wbuf.at[position % 2], wsem.at[position % 2]
        )

    load(0).start()
    own_cot = pltpu.make_async_copy(cot, cotall.at[bs], kr.at[bs])
    own_cot.start()

    barrier = pltpu.get_barrier_semaphore()
    for d in range(1, G):
        pl.semaphore_signal(
            barrier, inc=1, device_id=plane(lax.rem(bs + d, G)), device_id_type=MESH
        )

    @pl.when(m > 0)
    def _():
        pl.semaphore_signal(barrier, inc=1, device_id=below, device_id_type=MESH)

    @pl.when(m < M - 1)
    def _():
        pl.semaphore_signal(barrier, inc=1, device_id=above, device_id_type=MESH)

    edge = (m == 0) | (m == M - 1)

    @pl.when(edge)
    def _():
        pl.semaphore_wait(barrier, G)

    @pl.when(jnp.logical_not(edge))
    def _():
        pl.semaphore_wait(barrier, G + 1)

    def ctx_up(src, mm):
        return remote(src, zctx.at[mm], zu.at[mm], zr.at[mm], above)

    def ctx_down(src, mm):
        return remote(src, zctx.at[mm], zd.at[mm], zr.at[mm], below)

    def hand_out(src, mm):
        for h in range(Q):
            dest = mm * Q + h

            @pl.when(dest != bs)
            def _():
                remote(piece_of(src, h), ctxall.at[bs], cs.at[dest], cr.at[bs], plane(dest)).start()

            @pl.when(dest == bs)
            def _():
                pltpu.make_async_copy(piece_of(src, h), ctxall.at[bs], cr.at[bs]).start()

    @pl.when(m < M - 1)
    def _():
        ctx_up(ctx, m).start()

    @pl.when(m > 0)
    def _():
        ctx_down(ctx, m).start()

    def cot_send(dq):
        q = lax.rem(b * half + s // 2 + dq, B * half)
        dest = (q // half, lax.rem(q, half) * 2 + parity, m)
        return remote(cot, cotall.at[bs], ks.at[dq], kr.at[bs], dest)

    def cot_partner():
        return remote(cot, cotall.at[bs], ks.at[0], kr.at[bs], partner)

    def cot_from(dq):
        q = lax.rem(b * half + s // 2 + dq, B * half)
        return (q // half) * S + lax.rem(q, half) * 2 + parity

    def cot_forward(dq):
        j = cot_from(dq)
        return remote(cotall.at[j], cotall.at[j], kf.at[dq], kr.at[j], partner)

    cot_partner().start()
    hand_out(ctx, m)
    for dq in range(1, B * half):
        cot_send(dq).start()

    def chunk(ref, k, c):
        return ref.at[k, pl.ds(c * rows, rows), :]

    def sum_up(k, c):
        return remote(chunk(part, k, c), chunk(rup, k, c), pus.at[k, c], pur.at[k, c], above)

    def sum_down(k, c):
        return remote(chunk(part, k, c), chunk(rdn, k, c), pds.at[k, c], pdr.at[k, c], below)

    span = tile_of(width)

    def product(position):
        k = order[position]
        load(position).wait()
        if position + 1 < M:
            load(position + 1).start()

        @pl.loop(0, width // span)
        def _(t):
            cols = pl.ds(pl.multiple_of(t * span, span), span)
            part[k, :, cols] = lax.dot_general(
                cot[...], wbuf[position % 2, cols, :],
                (((1,), (1,)), ((), ())), preferred_element_type=jnp.float32,
            )

        @pl.when((m == 0) & (k > m))
        def _():
            for c in range(CHUNKS):
                sum_up(k, c).start()

        @pl.when((m == M - 1) & (k < m))
        def _():
            for c in range(CHUNKS):
                sum_down(k, c).start()

    def arrivals(r):
        @pl.when(m >= r)
        def _():
            mm = m - r
            ctx_up(zctx.at[mm], mm).wait_recv()

            @pl.when(m < M - 1)
            def _():
                ctx_up(zctx.at[mm], mm).start()

            hand_out(zctx.at[mm], mm)

        @pl.when(m + r < M)
        def _():
            mm = m + r
            ctx_down(zctx.at[mm], mm).wait_recv()

            @pl.when(m > 0)
            def _():
                ctx_down(zctx.at[mm], mm).start()

            hand_out(zctx.at[mm], mm)

    r = 1
    for position in range(M):
        product(position)
        if position % 2 == 1 and r < M:
            arrivals(r)
            r += 1
    for dq in range(1, B * half):
        j = cot_from(dq)
        remote(cotall.at[j], cotall.at[j], kf.at[dq], kr.at[j], partner).wait_recv()
        cot_forward(dq).start()
    while r < M:
        arrivals(r)
        r += 1

    for j in range(M - 1):
        up, down = M - 1 - j, j

        @pl.when((m > 0) & (m < up))
        def _():
            for c in range(CHUNKS):
                sum_up(up, c).wait_recv()
                piece = pl.ds(c * rows, rows)
                part[up, piece, :] += rup[up, piece, :]
                sum_up(up, c).start()

        @pl.when((m < M - 1) & (m > down))
        def _():
            for c in range(CHUNKS):
                sum_down(down, c).wait_recv()
                piece = pl.ds(c * rows, rows)
                part[down, piece, :] += rdn[down, piece, :]
                sum_down(down, c).start()

    own_cot.wait()
    for d in range(1, G):
        j = lax.rem(bs + d, G)
        remote(ctxall.at[j], ctxall.at[j], cs.at[j], cr.at[j], partner).wait_recv()
    pltpu.make_async_copy(ctxall.at[bs], ctxall.at[bs], cr.at[bs]).wait()
    remote(cotall.at[partner_bs], cotall.at[partner_bs], ks.at[0], kr.at[partner_bs], partner).wait_recv()
    for dq in range(1, B * half):
        j = cot_from(dq) + 1 - 2 * parity
        remote(cotall.at[j], cotall.at[j], kf.at[dq], kr.at[j], partner).wait_recv()

    for j in range(G):
        ctxt[:, j * T : (j + 1) * T] = ctxall[j].T
    gspan = tile_of(width)

    @pl.loop(0, width // gspan)
    def _(t):
        cols = pl.ds(pl.multiple_of(t * gspan, gspan), gspan)
        gw[:, cols] = jnp.dot(
            ctxt[...], cotall[:, :, cols].reshape(G * T, gspan),
            preferred_element_type=jnp.float32,
        )

    for c in range(CHUNKS):
        piece = pl.ds(c * rows, rows)

        @pl.when(m > 0)
        def _():
            sum_up(m, c).wait_recv()
            part[m, piece, :] += rup[m, piece, :]

        @pl.when(m < M - 1)
        def _():
            sum_down(m, c).wait_recv()
            part[m, piece, :] += rdn[m, piece, :]

        gc[piece, :] = part[m, piece, :].astype(gc.dtype)

    for mm in range(M):
        @pl.when((m < M - 1) & (mm <= m))
        def _():
            ctx_up(ctx, mm).wait_send()

        @pl.when((m > 0) & (mm >= m))
        def _():
            ctx_down(ctx, mm).wait_send()

        for c in range(CHUNKS):
            @pl.when(mm > m)
            def _():
                sum_up(mm, c).wait_send()

            @pl.when(mm < m)
            def _():
                sum_down(mm, c).wait_send()

    for dest in range(G):
        @pl.when(dest != bs)
        def _():
            remote(piece_of(ctx, 0), ctxall.at[bs], cs.at[dest], cr.at[bs], partner).wait_send()

    cot_partner().wait_send()
    for dq in range(1, B * half):
        cot_send(dq).wait_send()
        cot_forward(dq).wait_send()


def shards(context, cotangent, out_weight):
    B, S, M = lax.axis_size("batch"), lax.axis_size("seq"), lax.axis_size("mp")
    G = B * S
    T, width = cotangent.shape
    Q = G // M
    F = context.shape[1] // Q
    pieces = context
    if F % 128:
        pieces = jnp.stack([context[:, h * F : (h + 1) * F] for h in range(Q)])
    pairs = B * (S // 2)
    dma = pltpu.SemaphoreType.DMA
    vmem = pl.BlockSpec(memory_space=pltpu.VMEM)
    return pl.pallas_call(
        functools.partial(kernel, B, S, M),
        out_shape=(
            jax.ShapeDtypeStruct((F, width), jnp.float32),
            jax.ShapeDtypeStruct((T, context.shape[1]), jnp.bfloat16),
        ),
        in_specs=[vmem, vmem, pl.BlockSpec(memory_space=pl.ANY)],
        out_specs=(vmem, vmem),
        scratch_shapes=[
            pltpu.VMEM((M, *pieces.shape), jnp.bfloat16),
            pltpu.VMEM((G, T, width), jnp.bfloat16),
            pltpu.VMEM((G, T, F), jnp.bfloat16),
            pltpu.VMEM((F, G * T), jnp.bfloat16),
            pltpu.VMEM((M, T, width), jnp.float32),
            pltpu.VMEM((M, T, width), jnp.float32),
            pltpu.VMEM((M, T, width), jnp.float32),
            pltpu.VMEM((2, width, width), jnp.bfloat16),
            dma((2,)), dma((M,)), dma((M,)), dma((M,)),
            dma((G,)), dma((G,)), dma((pairs,)), dma((pairs,)), dma((G,)),
            dma((M, CHUNKS)), dma((M, CHUNKS)), dma((M, CHUNKS)), dma((M, CHUNKS)),
        ],
        compiler_params=pltpu.CompilerParams(collective_id=0, has_side_effects=True),
        name="output_projection_backward",
    )(pieces, cotangent, out_weight)


def solution(mesh):
    return jax.shard_map(
        shards,
        mesh=mesh,
        in_specs=(P(("batch", "seq"), "mp"), P(("batch", "seq"), "mp"), P(None, "mp")),
        out_specs=(P(("batch", "seq"), "mp"), P(("batch", "seq"), "mp")),
        check_vma=False,
    )
```

time: 177 us -> 102 us (0.58)
  the two profiles are of different devices: /device:TPU:16 before, /device:TPU:20 now
where the time goes in v1:
time: 102 us
  Pallas kernels  96 us (94%)
  local copies, waits for them, and re-layouts  5.64 us (6%)
    pallas_call x1, Pallas kernels, shards(): pl.pallas_call(functools.partial(kernel, B, S, M), out_shape=(jax.ShapeDt...  96 us
    unnamed x4, local copies, waits for them, and re-layouts  5.64 us

profile of v1, /device:TPU:20, one launch (start us, length us, event | category | flops | bytes accessed | tf_op | source)
XLA Modules:
  0.0 102.3 jit_solution(4577772876743060561)
XLA Ops:
  0.6 96.0 %output_projection_backward.1 = (f32[768,1536]{1,0:T(8,128)}, bf16[128,1536]{1,0:T(8,128)(2,1)}) custom-call(bf16[128,1536]{1,0:T(8,128)(2,1)} %ctx.1, bf16[128,1536]{1,0:T(8,128)(2,1)} %cot.1, bf16[6144,1536]{1,0:T(8,128)(2,1)} %w.1), custom_call_target="tpu_custom_call" | custom-call | tf_op jit(solution)/shard_map/output_projection_backward/pallas_call | solution.py:306
  96.6 0.0 copy-start
  96.6 4.9 %copy.7 = f32[768,1536]{1,0:T(8,128)} copy(f32[768,1536]{1,0:T(8,128)} %get-tuple-element.4) | data formatting | bytes 9437184
  101.5 0.0 copy-done
  101.5 0.7 copy.8
Async XLA Ops:
  96.6 4.9 %copy-start = (bf16[128,1536]{1,0:T(8,128)(2,1)S(1)}, bf16[128,1536]{1,0:T(8,128)(2,1)}, u32[]{:S(2)}) copy-start(bf16[128,1536]{1,0:T(8,128)(2,1)} %get-tuple-element.5) | copy-start | bytes 1179652

commit v2 on v1

--- a/solution.py
+++ b/solution.py
@@ -47,14 +47,13 @@
             device_id=device, device_id_type=MESH,
         )
 
-    order = []
-    for step in range((M + 1) // 2):
-        order.append(M - 1 - step)
-        if step != M - 1 - step:
-            order.append(step)
+    low = 2 * m < M
+
+    def target(position):
+        return jnp.where(low, M - 1 - position, position)
 
     def load(position):
-        k = order[position]
+        k = target(position)
         return pltpu.make_async_copy(
             w.at[pl.ds(k * width, width), :], wbuf.at[position % 2], wsem.at[position % 2]
         )
@@ -130,9 +129,9 @@
         return remote(cotall.at[j], cotall.at[j], kf.at[dq], kr.at[j], partner)
 
     cot_partner().start()
-    hand_out(ctx, m)
     for dq in range(1, B * half):
         cot_send(dq).start()
+    hand_out(ctx, m)
 
     def chunk(ref, k, c):
         return ref.at[k, pl.ds(c * rows, rows), :]
@@ -146,7 +145,7 @@
     span = tile_of(width)
 
     def product(position):
-        k = order[position]
+        k = target(position)
         load(position).wait()
         if position + 1 < M:
             load(position + 1).start()
@@ -192,12 +191,38 @@
 
             hand_out(zctx.at[mm], mm)
 
+    def pass_up(k, c):
+        piece = pl.ds(c * rows, rows)
+        sum_up(k, c).wait_recv()
+        part[k, piece, :] += rup[k, piece, :]
+        sum_up(k, c).start()
+
+    def pass_down(k, c):
+        piece = pl.ds(c * rows, rows)
+        sum_down(k, c).wait_recv()
+        part[k, piece, :] += rdn[k, piece, :]
+        sum_down(k, c).start()
+
+    def chain(tick):
+        up = M - 1 - (tick - m)
+        down = tick - (M - 1 - m)
+        for c in range(CHUNKS):
+            @pl.when((m > 0) & (m < up) & (up < M))
+            def _():
+                pass_up(up, c)
+
+            @pl.when((m < M - 1) & (m > down) & (down >= 0))
+            def _():
+                pass_down(down, c)
+
     r = 1
     for position in range(M):
         product(position)
         if position % 2 == 1 and r < M:
             arrivals(r)
             r += 1
+    if M > 2:
+        chain(1)
     for dq in range(1, B * half):
         j = cot_from(dq)
         remote(cotall.at[j], cotall.at[j], kf.at[dq], kr.at[j], partner).wait_recv()
@@ -205,25 +230,8 @@
     while r < M:
         arrivals(r)
         r += 1
-
-    for j in range(M - 1):
-        up, down = M - 1 - j, j
-
-        @pl.when((m > 0) & (m < up))
-        def _():
-            for c in range(CHUNKS):
-                sum_up(up, c).wait_recv()
-                piece = pl.ds(c * rows, rows)
-                part[up, piece, :] += rup[up, piece, :]
-                sum_up(up, c).start()
-
-        @pl.when((m < M - 1) & (m > down))
-        def _():
-            for c in range(CHUNKS):
-                sum_down(down, c).wait_recv()
-                piece = pl.ds(c * rows, rows)
-                part[down, piece, :] += rdn[down, piece, :]
-                sum_down(down, c).start()
+    for tick in range(2, M - 1):
+        chain(tick)
 
     own_cot.wait()
     for d in range(1, G):

time: 102 us -> 74.9 us (0.73)
  the two profiles are of different devices: /device:TPU:20 before, /device:TPU:16 now
where the time goes in v2:
time: 74.9 us; the launch traced here: 74.7 us
  Pallas kernels  68.4 us (91%)
  local copies, waits for them, and re-layouts  5.64 us (8%)
    pallas_call x1, Pallas kernels, shards(): pl.pallas_call(functools.partial(kernel, B, S, M), out_shape=(jax.ShapeDt...  68.4 us
    unnamed x4, local copies, waits for them, and re-layouts  5.64 us

profile of v2, /device:TPU:16, one launch (start us, length us, event | category | flops | bytes accessed | tf_op | source)
XLA Modules:
  0.0 74.7 jit_solution(12289750530232402943)
XLA Ops:
  0.6 68.4 %output_projection_backward.1 = (f32[768,1536]{1,0:T(8,128)}, bf16[128,1536]{1,0:T(8,128)(2,1)}) custom-call(bf16[128,1536]{1,0:T(8,128)(2,1)} %ctx.1, bf16[128,1536]{1,0:T(8,128)(2,1)} %cot.1, bf16[6144,1536]{1,0:T(8,128)(2,1)} %w.1), custom_call_target="tpu_custom_call" | custom-call | tf_op jit(solution)/shard_map/output_projection_backward/pallas_call | solution.py:314
  69.0 0.0 copy-start
  69.1 4.9 %copy.7 = f32[768,1536]{1,0:T(8,128)} copy(f32[768,1536]{1,0:T(8,128)} %get-tuple-element.4) | data formatting | bytes 9437184
  73.9 0.0 copy-done
  74.0 0.7 copy.8
Async XLA Ops:
  69.0 4.9 %copy-start = (bf16[128,1536]{1,0:T(8,128)(2,1)S(1)}, bf16[128,1536]{1,0:T(8,128)(2,1)}, u32[]{:S(2)}) copy-start(bf16[128,1536]{1,0:T(8,128)(2,1)} %get-tuple-element.5) | copy-start | bytes 1179652

commit v3 on v2

--- a/solution.py
+++ b/solution.py
@@ -332,7 +332,7 @@
             dma((G,)), dma((G,)), dma((pairs,)), dma((pairs,)), dma((G,)),
             dma((M, CHUNKS)), dma((M, CHUNKS)), dma((M, CHUNKS)), dma((M, CHUNKS)),
         ],
-        compiler_params=pltpu.CompilerParams(collective_id=0, has_side_effects=True),
+        compiler_params=pltpu.CompilerParams(collective_id=0, has_side_effects=True, vmem_limit_bytes=44 * 1024 * 1024),
         name="output_projection_backward",
     )(pieces, cotangent, out_weight)
 

time: 74.9 us -> 70.8 us (0.945)
  Pallas kernels: 68.4 us -> 65 us
    pallas_call x1, Pallas kernels: 68.4 us -> 65 us  [shards(): pl.pallas_call(functools.partial(kernel, B, S, M), out_shape=(jax.ShapeDt...]
    unnamed x4 -> x6, local copies, waits for them, and re-layouts: 5.64 us -> 4.92 us
where the time goes in v3:
time: 70.8 us; the launch traced here: 70.6 us
  Pallas kernels  65 us (92%)
  local copies, waits for them, and re-layouts  4.92 us (7%)
    pallas_call x1, Pallas kernels, shards(): pl.pallas_call(functools.partial(kernel, B, S, M), out_shape=(jax.ShapeDt...  65 us
    unnamed x6, local copies, waits for them, and re-layouts  4.92 us

profile of v3, /device:TPU:16, one launch (start us, length us, event | category | flops | bytes accessed | tf_op | source)
XLA Modules:
  0.0 70.6 jit_solution(7050905510505277766)
XLA Ops:
  0.6 0.0 copy-start
  0.6 1.0 %copy-done = bf16[128,1536]{1,0:T(8,128)(2,1)S(1)} copy-done((bf16[128,1536]{1,0:T(8,128)(2,1)S(1)}, bf16[128,1536]{1,0:T(8,128)(2,1)}, u32[]{:S(2)}) %copy-start) | copy-done | bytes 393240
  1.6 0.0 copy-start.1
  1.6 1.0 %copy-done.1 = bf16[128,1536]{1,0:T(8,128)(2,1)S(1)} copy-done((bf16[128,1536]{1,0:T(8,128)(2,1)S(1)}, bf16[128,1536]{1,0:T(8,128)(2,1)}, u32[]{:S(2)}) %copy-start.1) | copy-done | bytes 393240
  2.6 65.0 %output_projection_backward.1 = (f32[768,1536]{1,0:T(8,128)S(1)}, bf16[128,1536]{1,0:T(8,128)(2,1)S(1)}) custom-call(bf16[128,1536]{1,0:T(8,128)(2,1)S(1)} %copy-done, bf16[128,1536]{1,0:T(8,128)(2,1)S(1)} %copy-done.1, bf16[6144,1536]{1,0:T(8,128)(2,1)} %w.1), custom_call_target="tpu_custom_call" | custom-call | tf_op jit(solution)/shard_map/output_projection_backward/pallas_call | solution.py:314
  67.6 2.2 %copy.7 = f32[768,1536]{1,0:T(8,128)} copy(f32[768,1536]{1,0:T(8,128)S(1)} %get-tuple-element.4) | data formatting | bytes 9437184
  69.8 0.7 %copy.8 = bf16[128,1536]{1,0:T(8,128)(2,1)} copy(bf16[128,1536]{1,0:T(8,128)(2,1)S(1)} %get-tuple-element.5) | data formatting | bytes 786432
Async XLA Ops:
  0.6 1.0 %copy-start = (bf16[128,1536]{1,0:T(8,128)(2,1)S(1)}, bf16[128,1536]{1,0:T(8,128)(2,1)}, u32[]{:S(2)}) copy-start(bf16[128,1536]{1,0:T(8,128)(2,1)} %ctx.1) | copy-start | bytes 1179652
  1.6 1.0 %copy-start.1 = (bf16[128,1536]{1,0:T(8,128)(2,1)S(1)}, bf16[128,1536]{1,0:T(8,128)(2,1)}, u32[]{:S(2)}) copy-start(bf16[128,1536]{1,0:T(8,128)(2,1)} %cot.1) | copy-start | bytes 1179652

commit v4 on v3

--- a/solution.py
+++ b/solution.py
@@ -9,6 +9,9 @@
 
 MESH = pl.DeviceIdType.MESH
 CHUNKS = 2
+PARTS = 4
+LEVELS = 36
+BASE = 75
 
 
 def tile_of(width):
@@ -18,7 +21,7 @@
 def kernel(
     B, S, M,
     ctx, cot, w, gw, gc,
-    zctx, cotall, ctxall, ctxt, part, rup, rdn, wbuf,
+    zctx, cotall, ctxall, ctxt, part, rup, rdn, high, low_bits, hup, lup, hdn, ldn, wbuf,
     wsem, zr, zu, zd, cs, cr, ks, kf, kr, pus, pds, pur, pdr,
 ):
     G = B * S
@@ -136,11 +139,100 @@
     def chunk(ref, k, c):
         return ref.at[k, pl.ds(c * rows, rows), :]
 
-    def sum_up(k, c):
-        return remote(chunk(part, k, c), chunk(rup, k, c), pus.at[k, c], pur.at[k, c], above)
-
-    def sum_down(k, c):
-        return remote(chunk(part, k, c), chunk(rdn, k, c), pds.at[k, c], pdr.at[k, c], below)
+    quarter = rows // PARTS
+    ups = (above, pus, pur, rup, hup, lup)
+    downs = (below, pds, pdr, rdn, hdn, ldn)
+
+    def short(ref, k, c):
+        return ref.at[k, pl.ds(c * quarter, quarter), :]
+
+    def plain(way, k, c):
+        device, send, recv, full, _, _ = way
+        return remote(chunk(part, k, c), chunk(full, k, c), send.at[k, c, 0], recv.at[k, c, 0], device)
+
+    def coded(way, k, c):
+        device, send, recv, _, rhigh, rlow = way
+        return (
+            remote(chunk(high, k, c), chunk(rhigh, k, c), send.at[k, c, 0], recv.at[k, c, 0], device),
+            remote(short(low_bits, k, c), short(rlow, k, c), send.at[k, c, 1], recv.at[k, c, 1], device),
+        )
+
+    def is_coded(way, sender, k):
+        if way is ups:
+            return (sender == 0) | ((k == M - 1) & (sender < M - 2))
+        return (sender == M - 1) | ((k == 0) & (sender > 1))
+
+    def encode(k, c):
+        @pl.loop(0, width // span)
+        def _(t):
+            cols = pl.ds(pl.multiple_of(t * span, span), span)
+            total = None
+            for i in range(PARTS):
+                lines = pl.ds(c * rows + i * quarter, quarter)
+                value = part[k, lines, cols]
+                top = value.astype(jnp.bfloat16)
+                high[k, lines, cols] = top
+                top = top.astype(jnp.float32)
+                size = jnp.abs(top)
+                usable = size > 1e-30
+                scale = (256.0 * LEVELS) / jnp.where(usable, size, 1.0)
+                rest = jnp.floor(jnp.where(usable, (value - top) * scale, 0.0) + 0.5)
+                total = rest if total is None else total * BASE + rest
+            low_bits[k, pl.ds(c * quarter, quarter), cols] = total
+
+    def decode(rhigh, rlow, k, c):
+        @pl.loop(0, width // span)
+        def _(t):
+            cols = pl.ds(pl.multiple_of(t * span, span), span)
+            left = rlow[k, pl.ds(c * quarter, quarter), cols]
+            for i in range(PARTS):
+                lines = pl.ds(c * rows + i * quarter, quarter)
+                unit = float(BASE ** (PARTS - 1 - i))
+                rest = jnp.floor(left * (1.0 / unit) + 0.5)
+                left = left - rest * unit
+                top = rhigh[k, lines, cols].astype(jnp.float32)
+                value = top + rest * (jnp.abs(top) * (1.0 / (256.0 * LEVELS)))
+                part[k, lines, cols] += value
+
+    def send_sum(way, k, c):
+        code = is_coded(way, m, k)
+
+        @pl.when(code)
+        def _():
+            encode(k, c)
+            for copy in coded(way, k, c):
+                copy.start()
+
+        @pl.when(jnp.logical_not(code))
+        def _():
+            plain(way, k, c).start()
+
+    def sent_sum(way, k, c):
+        code = is_coded(way, m, k)
+
+        @pl.when(code)
+        def _():
+            for copy in coded(way, k, c):
+                copy.wait_send()
+
+        @pl.when(jnp.logical_not(code))
+        def _():
+            plain(way, k, c).wait_send()
+
+    def take_sum(way, k, c):
+        code = is_coded(way, m - 1 if way is ups else m + 1, k)
+
+        @pl.when(code)
+        def _():
+            for copy in coded(way, k, c):
+                copy.wait_recv()
+            decode(way[4], way[5], k, c)
+
+        @pl.when(jnp.logical_not(code))
+        def _():
+            plain(way, k, c).wait_recv()
+            piece = pl.ds(c * rows, rows)
+            part[k, piece, :] += way[3][k, piece, :]
 
     span = tile_of(width)
 
@@ -161,12 +253,12 @@
         @pl.when((m == 0) & (k > m))
         def _():
             for c in range(CHUNKS):
-                sum_up(k, c).start()
+                send_sum(ups, k, c)
 
         @pl.when((m == M - 1) & (k < m))
         def _():
             for c in range(CHUNKS):
-                sum_down(k, c).start()
+                send_sum(downs, k, c)
 
     def arrivals(r):
         @pl.when(m >= r)
@@ -191,17 +283,9 @@
 
             hand_out(zctx.at[mm], mm)
 
-    def pass_up(k, c):
-        piece = pl.ds(c * rows, rows)
-        sum_up(k, c).wait_recv()
-        part[k, piece, :] += rup[k, piece, :]
-        sum_up(k, c).start()
-
-    def pass_down(k, c):
-        piece = pl.ds(c * rows, rows)
-        sum_down(k, c).wait_recv()
-        part[k, piece, :] += rdn[k, piece, :]
-        sum_down(k, c).start()
+    def pass_on(way, k, c):
+        take_sum(way, k, c)
+        send_sum(way, k, c)
 
     def chain(tick):
         up = M - 1 - (tick - m)
@@ -209,11 +293,11 @@
         for c in range(CHUNKS):
             @pl.when((m > 0) & (m < up) & (up < M))
             def _():
-                pass_up(up, c)
+                pass_on(ups, up, c)
 
             @pl.when((m < M - 1) & (m > down) & (down >= 0))
             def _():
-                pass_down(down, c)
+                pass_on(downs, down, c)
 
     r = 1
     for position in range(M):
@@ -260,13 +344,11 @@
 
         @pl.when(m > 0)
         def _():
-            sum_up(m, c).wait_recv()
-            part[m, piece, :] += rup[m, piece, :]
+            take_sum(ups, m, c)
 
         @pl.when(m < M - 1)
         def _():
-            sum_down(m, c).wait_recv()
-            part[m, piece, :] += rdn[m, piece, :]
+            take_sum(downs, m, c)
 
         gc[piece, :] = part[m, piece, :].astype(gc.dtype)
 
@@ -282,11 +364,11 @@
         for c in range(CHUNKS):
             @pl.when(mm > m)
             def _():
-                sum_up(mm, c).wait_send()
+                sent_sum(ups, mm, c)
 
             @pl.when(mm < m)
             def _():
-                sum_down(mm, c).wait_send()
+                sent_sum(downs, mm, c)
 
     for dest in range(G):
         @pl.when(dest != bs)
@@ -327,12 +409,18 @@
             pltpu.VMEM((M, T, width), jnp.float32),
             pltpu.VMEM((M, T, width), jnp.float32),
             pltpu.VMEM((M, T, width), jnp.float32),
+            pltpu.VMEM((M, T, width), jnp.bfloat16),
+            pltpu.VMEM((M, T // PARTS, width), jnp.float32),
+            pltpu.VMEM((M, T, width), jnp.bfloat16),
+            pltpu.VMEM((M, T // PARTS, width), jnp.float32),
+            pltpu.VMEM((M, T, width), jnp.bfloat16),
+            pltpu.VMEM((M, T // PARTS, width), jnp.float32),
             pltpu.VMEM((2, width, width), jnp.bfloat16),
             dma((2,)), dma((M,)), dma((M,)), dma((M,)),
             dma((G,)), dma((G,)), dma((pairs,)), dma((pairs,)), dma((G,)),
-            dma((M, CHUNKS)), dma((M, CHUNKS)), dma((M, CHUNKS)), dma((M, CHUNKS)),
+            *[dma((M, CHUNKS, 2))] * 4,
         ],
-        compiler_params=pltpu.CompilerParams(collective_id=0, has_side_effects=True, vmem_limit_bytes=44 * 1024 * 1024),
+        compiler_params=pltpu.CompilerParams(collective_id=0, has_side_effects=True, vmem_limit_bytes=46 * 1024 * 1024),
         name="output_projection_backward",
     )(pieces, cotangent, out_weight)
 

time: 70.8 us -> 60.8 us (0.86)
  Pallas kernels: 65 us -> 55 us
    pallas_call x1, Pallas kernels: 65 us -> 55 us  [shards(): pl.pallas_call(functools.partial(kernel, B, S, M), out_shape=(jax.ShapeDt...]
where the time goes in v4:
time: 60.8 us; the launch traced here: 60.6 us
  Pallas kernels  55 us (90%)
  local copies, waits for them, and re-layouts  4.92 us (8%)
  between operations  0.65 us (1%)
    pallas_call x1, Pallas kernels, shards(): pl.pallas_call(functools.partial(kernel, B, S, M), out_shape=(jax.ShapeDt...  55 us
    unnamed x6, local copies, waits for them, and re-layouts  4.92 us

profile of v4, /device:TPU:16, one launch (start us, length us, event | category | flops | bytes accessed | tf_op | source)
XLA Modules:
  0.0 60.6 jit_solution(11741663900352325745)
XLA Ops:
  0.6 0.0 copy-start
  0.6 1.0 %copy-done = bf16[128,1536]{1,0:T(8,128)(2,1)S(1)} copy-done((bf16[128,1536]{1,0:T(8,128)(2,1)S(1)}, bf16[128,1536]{1,0:T(8,128)(2,1)}, u32[]{:S(2)}) %copy-start) | copy-done | bytes 393240
  1.6 0.0 copy-start.1
  1.6 1.0 %copy-done.1 = bf16[128,1536]{1,0:T(8,128)(2,1)S(1)} copy-done((bf16[128,1536]{1,0:T(8,128)(2,1)S(1)}, bf16[128,1536]{1,0:T(8,128)(2,1)}, u32[]{:S(2)}) %copy-start.1) | copy-done | bytes 393240
  2.6 55.0 %output_projection_backward.1 = (f32[768,1536]{1,0:T(8,128)S(1)}, bf16[128,1536]{1,0:T(8,128)(2,1)S(1)}) custom-call(bf16[128,1536]{1,0:T(8,128)(2,1)S(1)} %copy-done, bf16[128,1536]{1,0:T(8,128)(2,1)S(1)} %copy-done.1, bf16[6144,1536]{1,0:T(8,128)(2,1)} %w.1), custom_call_target="tpu_custom_call" | custom-call | tf_op jit(solution)/shard_map/output_projection_backward/pallas_call | solution.py:396
  57.6 2.2 %copy.7 = f32[768,1536]{1,0:T(8,128)} copy(f32[768,1536]{1,0:T(8,128)S(1)} %get-tuple-element.4) | data formatting | bytes 9437184
  59.8 0.7 %copy.8 = bf16[128,1536]{1,0:T(8,128)(2,1)} copy(bf16[128,1536]{1,0:T(8,128)(2,1)S(1)} %get-tuple-element.5) | data formatting | bytes 786432
Async XLA Ops:
  0.6 1.0 %copy-start = (bf16[128,1536]{1,0:T(8,128)(2,1)S(1)}, bf16[128,1536]{1,0:T(8,128)(2,1)}, u32[]{:S(2)}) copy-start(bf16[128,1536]{1,0:T(8,128)(2,1)} %ctx.1) | copy-start | bytes 1179652
  1.6 1.0 %copy-start.1 = (bf16[128,1536]{1,0:T(8,128)(2,1)S(1)}, bf16[128,1536]{1,0:T(8,128)(2,1)}, u32[]{:S(2)}) copy-start(bf16[128,1536]{1,0:T(8,128)(2,1)} %cot.1) | copy-start | bytes 1179652

commit v5 on v4

--- a/solution.py
+++ b/solution.py
@@ -157,10 +157,10 @@
             remote(short(low_bits, k, c), short(rlow, k, c), send.at[k, c, 1], recv.at[k, c, 1], device),
         )
 
-    def is_coded(way, sender, k):
+    def is_coded(way, sender):
         if way is ups:
-            return (sender == 0) | ((k == M - 1) & (sender < M - 2))
-        return (sender == M - 1) | ((k == 0) & (sender > 1))
+            return (sender == 0) | (sender < M - 2)
+        return (sender == M - 1) | (sender > 1)
 
     def encode(k, c):
         @pl.loop(0, width // span)
@@ -195,7 +195,7 @@
                 part[k, lines, cols] += value
 
     def send_sum(way, k, c):
-        code = is_coded(way, m, k)
+        code = is_coded(way, m)
 
         @pl.when(code)
         def _():
@@ -208,7 +208,7 @@
             plain(way, k, c).start()
 
     def sent_sum(way, k, c):
-        code = is_coded(way, m, k)
+        code = is_coded(way, m)
 
         @pl.when(code)
         def _():
@@ -220,7 +220,7 @@
             plain(way, k, c).wait_send()
 
     def take_sum(way, k, c):
-        code = is_coded(way, m - 1 if way is ups else m + 1, k)
+        code = is_coded(way, m - 1 if way is ups else m + 1)
 
         @pl.when(code)
         def _():
@@ -246,7 +246,7 @@
         def _(t):
             cols = pl.ds(pl.multiple_of(t * span, span), span)
             part[k, :, cols] = lax.dot_general(
-                cot[...], wbuf[position % 2, cols, :],
+                cotall[bs], wbuf[position % 2, cols, :],
                 (((1,), (1,)), ((), ())), preferred_element_type=jnp.float32,
             )
 
@@ -259,6 +259,8 @@
         def _():
             for c in range(CHUNKS):
                 send_sum(downs, k, c)
+
+    own_cot.wait()
 
     def arrivals(r):
         @pl.when(m >= r)
@@ -317,7 +319,6 @@
     for tick in range(2, M - 1):
         chain(tick)
 
-    own_cot.wait()
     for d in range(1, G):
         j = lax.rem(bs + d, G)
         remote(ctxall.at[j], ctxall.at[j], cs.at[j], cr.at[j], partner).wait_recv()
@@ -393,13 +394,14 @@
     pairs = B * (S // 2)
     dma = pltpu.SemaphoreType.DMA
     vmem = pl.BlockSpec(memory_space=pltpu.VMEM)
+    hbm = pl.BlockSpec(memory_space=pltpu.HBM)
     return pl.pallas_call(
         functools.partial(kernel, B, S, M),
         out_shape=(
             jax.ShapeDtypeStruct((F, width), jnp.float32),
             jax.ShapeDtypeStruct((T, context.shape[1]), jnp.bfloat16),
         ),
-        in_specs=[vmem, vmem, pl.BlockSpec(memory_space=pl.ANY)],
+        in_specs=[hbm, hbm, hbm],
         out_specs=(vmem, vmem),
         scratch_shapes=[
             pltpu.VMEM((M, *pieces.shape), jnp.bfloat16),

time: 60.8 us -> 59.4 us (0.977); the launches traced: 60.6 us -> 58.4 us
  Pallas kernels: 55 us -> 52.8 us
    pallas_call x1, Pallas kernels: 55 us -> 52.8 us  [shards(): pl.pallas_call(functools.partial(kernel, B, S, M), out_shape=(jax.ShapeDt...]
where the time goes in v5:
time: 59.4 us; the launch traced here: 58.4 us
  Pallas kernels  52.8 us (89%)
  local copies, waits for them, and re-layouts  4.92 us (8%)
  between operations  0.65 us (1%)
    pallas_call x1, Pallas kernels, shards(): pl.pallas_call(functools.partial(kernel, B, S, M), out_shape=(jax.ShapeDt...  52.8 us
    unnamed x6, local copies, waits for them, and re-layouts  4.92 us

profile of v5, /device:TPU:16, one launch (start us, length us, event | category | flops | bytes accessed | tf_op | source)
XLA Modules:
  0.0 58.4 jit_solution(1772785755512975405)
XLA Ops:
  0.6 0.0 copy-start
  0.6 1.0 %copy-done = bf16[128,1536]{1,0:T(8,128)(2,1)S(1)} copy-done((bf16[128,1536]{1,0:T(8,128)(2,1)S(1)}, bf16[128,1536]{1,0:T(8,128)(2,1)}, u32[]{:S(2)}) %copy-start) | copy-done | bytes 393240
  1.6 0.0 copy-start.1
  1.6 1.0 %copy-done.1 = bf16[128,1536]{1,0:T(8,128)(2,1)S(1)} copy-done((bf16[128,1536]{1,0:T(8,128)(2,1)S(1)}, bf16[128,1536]{1,0:T(8,128)(2,1)}, u32[]{:S(2)}) %copy-start.1) | copy-done | bytes 393240
  2.6 52.8 %output_projection_backward.1 = (f32[768,1536]{1,0:T(8,128)S(1)}, bf16[128,1536]{1,0:T(8,128)(2,1)S(1)}) custom-call(bf16[128,1536]{1,0:T(8,128)(2,1)S(1)} %copy-done, bf16[128,1536]{1,0:T(8,128)(2,1)S(1)} %copy-done.1, bf16[6144,1536]{1,0:T(8,128)(2,1)} %w.1), custom_call_target="tpu_custom_call" | custom-call | tf_op jit(solution)/shard_map/output_projection_backward/pallas_call | solution.py:398
  55.5 2.2 %copy.7 = f32[768,1536]{1,0:T(8,128)} copy(f32[768,1536]{1,0:T(8,128)S(1)} %get-tuple-element.4) | data formatting | bytes 9437184
  57.6 0.7 %copy.8 = bf16[128,1536]{1,0:T(8,128)(2,1)} copy(bf16[128,1536]{1,0:T(8,128)(2,1)S(1)} %get-tuple-element.5) | data formatting | bytes 786432
Async XLA Ops:
  0.6 1.0 %copy-start = (bf16[128,1536]{1,0:T(8,128)(2,1)S(1)}, bf16[128,1536]{1,0:T(8,128)(2,1)}, u32[]{:S(2)}) copy-start(bf16[128,1536]{1,0:T(8,128)(2,1)} %ctx.1) | copy-start | bytes 1179652
  1.6 1.0 %copy-start.1 = (bf16[128,1536]{1,0:T(8,128)(2,1)S(1)}, bf16[128,1536]{1,0:T(8,128)(2,1)}, u32[]{:S(2)}) copy-start(bf16[128,1536]{1,0:T(8,128)(2,1)} %cot.1) | copy-start | bytes 1179652
